TPU v7x, 32 devices: a whole 2x2x4 slice. The times are simulated.
32 devices in a mesh: state: 4 (over z), basis: 8 (over y, x, core).
Axes of the slice: x: 2, y: 2, z: 4, core: 2. Of those that a mesh axis runs over, the one named last changes fastest.
Arguments:
- states: float32 [8, 64, 64000], P('state', 'basis'), may hold values from -40 to 40
- membrane_step: float32 [40, 40], replicated, may hold values from -1 to 1
- cavity_forward: float32 [64, 64], replicated, may hold values from -0.75 to 0.75
- coupling: float32 [64, 40], replicated, may hold values from 0.25 to 1
- membrane_forward: float32 [40, 40], replicated, may hold values from -1 to 1
- cavity_back: float32 [64, 64], replicated, may hold values from -9 to 9
- membrane_back: float32 [40, 40], replicated, may hold values from -1 to 1
Outputs:
- orthonormal: float32 [8, 64, 64000], P('state', 'basis')
All inputs are finite; a program needn't handle non-finite values.
Results may differ from a plain program's by a relative error of at most 0.000075.
Values sent between devices are 32-bit elements; how exact they have to be, the bound alone decides.
A program may use at most 192 MiB of HBM per device.

v0:
```python
import jax
import jax.numpy as jnp
from jax import lax
from jax.sharding import PartitionSpec as P


def body(
    states, membrane_step, cavity_forward, coupling, membrane_forward, cavity_back, membrane_back
):
    highest = lax.Precision.HIGHEST
    panel_size, level_count, joint = states.shape
    levels_all = cavity_forward.shape[0]
    membrane_levels = membrane_step.shape[0]
    basis_total = float(levels_all * joint)
    head = jnp.einsum(
        "ab,scbr->scar",
        membrane_step,
        states.reshape(panel_size, level_count, membrane_levels, joint // membrane_levels),
        precision=highest,
    )
    head = head.reshape(panel_size, level_count, joint)
    panel_block = lax.all_to_all(head, "basis", split_axis=2, concat_axis=1, tiled=True)
    items, cavity_all, columns = panel_block.shape
    grid = jnp.einsum("qc,kcr->kqr", cavity_forward, panel_block, precision=highest)
    grid = jnp.einsum(
        "kqtm,nm->kqtn",
        grid.reshape(items, cavity_all, columns // membrane_levels, membrane_levels),
        membrane_forward,
        precision=highest,
    )
    weighted = grid * coupling[None, :, None, :]
    backward = jnp.einsum("kqtn,mn->kqtm", weighted, membrane_back, precision=highest)
    backward = backward.reshape(items, cavity_all, columns)
    stepped = jnp.einsum("cq,kqr->kcr", cavity_back, backward, precision=highest)
    spread = lax.all_to_all(stepped, "state", split_axis=2, concat_axis=0, tiled=True)
    state_total, spread_levels, spread_cols = spread.shape
    flattened = spread.reshape(state_total, -1)
    partial_gram = jnp.dot(flattened, flattened.T, precision=highest)
    gram = lax.psum(partial_gram, ("state", "basis")) / basis_total
    lower_factor = jnp.linalg.cholesky(gram)
    identity = jnp.eye(state_total, dtype=gram.dtype)
    inverse = lax.linalg.triangular_solve(lower_factor, identity, left_side=True, lower=True)
    local_result = jnp.dot(inverse, flattened, precision=highest)
    local_result = local_result.reshape(state_total, spread_levels, spread_cols)
    return lax.all_to_all(
        lax.all_to_all(local_result, "state", split_axis=0, concat_axis=2, tiled=True),
        "basis",
        split_axis=1,
        concat_axis=2,
        tiled=True,
    )


def solution(mesh):
    in_specs = (P("state", "basis", None), P(), P(), P(), P(), P(), P())
    out_specs = P("state", "basis", None)
    return jax.shard_map(body, mesh=mesh, in_specs=in_specs, out_specs=out_specs, check_vma=False)
```

profile of v0, /device:TPU:9, one launch (start us, length us, event | category | flops | bytes accessed | tf_op | source)
XLA Modules:
  0.0 943.0 jit_solution(17978958401633566701)
XLA Ops:
  0.0 0.0 copy-start
  0.0 0.0 copy-start.3
  0.0 4.5 reshape.28
  4.5 0.0 copy-done.3
  4.5 8.0 convolution_bitcast_fusion.2
  12.4 49.2 %copy.60 = f32[2,8,40,1600]{1,0,3,2:T(2,128)} copy(f32[2,8,40,1600]{3,2,1,0:T(8,128)} %convolution_bitcast_fusion.2) | data formatting | bytes 8192000 | tf_op jit(solution)/shard_map/reshape | solution.py:21
  61.6 136.9 %reshape.39 = f32[8,1,128000]{2,1,0:T(1,128)} reshape(f32[64000,2,8]{2,1,0:T(2,128)} %bitcast.76) | data formatting | bytes 8192000
  198.5 0.0 copy-start.6
  198.5 5.2 all-to-all-start
  203.7 0.0 copy-done.6
  203.7 0.1 copy.41
  203.8 44.5 %all-to-all-done = f32[8,1,128000]{2,1,0:T(1,128)} async-done(((f32[8,1,128000]{2,1,0:T(1,128)}), f32[8,1,128000]{2,1,0:T(1,128)}, u32[]{:S(2)}, u32[]{:S(2)}) %all-to-all-start) | async-done | bytes 4096032 | tf_op jit(solution)/shard_map/all_to_all | solution.py:22
  248.3 0.5 broadcast.49
  248.8 13.7 %reduce.6 = f32[8,128000]{1,0:T(8,128)} reduce(f32[8,1,128000]{2,1,0:T(1,128)} %all-to-all-done, f32[]{:T(128)} %broadcast.49), dimensions={1}, to_apply=%all_to_all.50.reduce_sub_computation | reduce | bytes 8192004 | tf_op jit(solution)/shard_map/all_to_all | solution.py:22
  262.5 142.2 %reshape.40 = f32[64000,2,8]{2,1,0:T(2,128)} reshape(f32[8,128000]{1,0:T(8,128)} %reduce.6) | data formatting | bytes 8192000
  404.6 71.1 %copy.38 = f32[2,8,8,8000]{3,1,2,0:T(8,128)} copy(f32[2,8,8,8000]{1,0,3,2:T(2,128)} %bitcast.77) | data formatting | bytes 8192000 | tf_op jit(solution)/shard_map/all_to_all | solution.py:22
  475.7 0.0 copy-done
  475.7 8.0 convolution_bitcast_fusion.1
  483.7 6.8 copy.39
  490.5 0.0 copy-start.4
  490.5 8.8 copy.40
  499.3 0.0 copy-done.4
  499.3 0.0 copy-start.5
  499.3 6.5 fusion.9
  505.9 0.0 copy-done.5
  505.9 7.2 fusion
  513.0 0.0 copy-start.2
  513.0 8.2 copy.42
  521.3 0.0 copy-done.2
  521.3 13.7 %convolution_bitcast_fusion = f32[2,64,8000]{2,1,0:T(8,128)} fusion(f32[2,64,8000]{1,2,0:T(8,128)} %bitcast.78, f32[64,64]{1,0:T(8,128)S(1)} %copy-done.2), kind=kOutput, calls=%fused_computation | convolution fusion | flops 786432000 | bytes 8208384 | tf_op jit(solution)/shard_map/cq,kqr->kcr/dot_general | solution.py:34
  535.0 10.7 %copy.44 = f32[2,64,8000]{1,0,2:T(2,128)} copy(f32[2,64,8000]{2,1,0:T(8,128)} %convolution_bitcast_fusion) | data formatting | bytes 8192000 | tf_op jit(solution)/shard_map/cq,kqr->kcr/transpose | solution.py:34
  545.6 11.5 %reshape.41 = f32[4,1,256000]{2,1,0:T(1,128)} reshape(f32[8000,2,64]{2,1,0:T(2,128)} %bitcast.81) | data formatting | bytes 8192000
  557.1 94.0 %all_to_all.69 = f32[4,1,256000]{2,1,0:T(1,128)} all-to-all(f32[4,1,256000]{2,1,0:T(1,128)} %reshape.41), channel_id=1, replica_groups=mesh['state'=4,'basis'=8] {'state'}, dimensions={0} | all-to-all | bytes 8192000 | tf_op jit(solution)/shard_map/all_to_all | solution.py:35
  651.1 14.4 %reduce.7 = f32[4,256000]{1,0:T(4,128)} reduce(f32[4,1,256000]{2,1,0:T(1,128)} %all_to_all.69, f32[]{:T(128)} %broadcast.49), dimensions={1}, to_apply=%all_to_all.54.reduce_sub_computation | reduce | bytes 8192004 | tf_op jit(solution)/shard_map/all_to_all | solution.py:35
  665.6 11.7 %reshape.42 = f32[8000,2,64]{2,1,0:T(2,128)} reshape(f32[4,256000]{1,0:T(4,128)} %reduce.7) | data formatting | bytes 8192000
  677.3 12.3 %copy.45 = f32[2,64,4,2000]{3,1,0,2:T(8,128)} copy(f32[2,64,4,2000]{1,0,3,2:T(2,128)} %bitcast.82) | data formatting | bytes 8192000 | tf_op jit(solution)/shard_map/all_to_all | solution.py:35
  689.6 7.5 reshape.32
  697.1 12.3 %fusion.15 = f32[8,8]{0,1:T(8,128)S(1)} fusion(f32[8,128000]{1,0:T(8,128)} %reshape.32), kind=kOutput, calls=%fused_computation.28 | convolution fusion | flops 98304000 | bytes 4096256 | tf_op jit(solution)/shard_map/dot_general | solution.py:38
  709.4 42.5 %psum.7 = f32[8,8]{0,1:T(8,128)S(1)} all-reduce(f32[8,8]{0,1:T(8,128)S(1)} %fusion.15), channel_id=1, replica_groups=mesh['state'=4,'basis'=8] {'state','basis'}, use_global_device_ids=true, to_apply=%region_0.0 | all-reduce | flops 64 | bytes 512 | tf_op jit(solution)/shard_map/psum | solution.py:39
  751.9 0.1 copy.47
  752.0 0.7 cholesky.17
  752.7 0.7 compare_reduce_fusion
  753.5 0.7 fusion.12
  754.2 0.6 custom-call.6
  754.8 0.2 convolution_bitcast_fusion.3
  755.0 7.5 dot_general.32
  762.4 7.8 fusion.2
  770.3 2.4 copy.50
  772.7 93.4 %all_to_all.70 = f32[8,64,2000]{2,1,0:T(8,128)S(1)} all-to-all(f32[8,64,2000]{2,1,0:T(8,128)S(1)} %copy.50), channel_id=1, replica_groups=mesh['state'=4,'basis'=8] {'state'}, dimensions={0} | all-to-all | bytes 8192000 | tf_op jit(solution)/shard_map/all_to_all | solution.py:46
  866.1 4.6 copy.65
  870.8 6.3 all_to_all.60
  877.1 5.4 copy.52
  882.4 53.1 %all_to_all.71 = f32[2,64,8000]{2,0,1:T(2,128)S(1)} all-to-all(f32[2,64,8000]{2,0,1:T(2,128)S(1)} %copy.52), channel_id=1, replica_groups=mesh['state'=4,'basis'=8] {'basis'}, dimensions={1} | all-to-all | bytes 8192000 | tf_op jit(solution)/shard_map/all_to_all | solution.py:45
  935.5 0.3 copy.66
  935.8 0.0 copy-start.1
  935.8 2.7 copy.54
  938.5 4.2 all_to_all.64
  942.7 0.0 copy-done.1
  (3 shorter events, 0.1 us)
Async XLA Ops:
  0.0 475.7 %copy-start = (f32[64,64]{1,0:T(8,128)S(1)}, f32[64,64]{1,0:T(8,128)}, u32[]{:S(2)}) copy-start(f32[64,64]{1,0:T(8,128)} %param.9) | copy-start | bytes 49156
  0.0 4.5 copy-start.3
  198.5 5.2 copy-start.6
  198.5 49.8 %all-to-all-start = ((f32[8,1,128000]{2,1,0:T(1,128)}), f32[8,1,128000]{2,1,0:T(1,128)}, u32[]{:S(2)}, u32[]{:S(2)}) async-start(f32[8,1,128000]{2,1,0:T(1,128)} %reshape.39), calls=%async_computation | async-start | bytes 8192000 | tf_op jit(solution)/shard_map/all_to_all | solution.py:22
  490.5 8.8 copy-start.4
  499.3 6.6 copy-start.5
  513.0 8.2 copy-start.2
  935.8 7.0 copy-start.1
where the time goes:
time: 958 us; the launch traced here: 943 us
  local copies, waits for them, and re-layouts  515 us (54%)
  blocking collectives  283 us (30%)
  matrix products  63.7 us (7%)
  waiting for transfers between devices  44.5 us (5%)
  other arithmetic  30.9 us (3%)
    unnamed x19, local copies, waits for them, and re-layouts  302 us
    all_to_all x1, blocking collectives, body(): lax.all_to_all(stepped, 'state', split_axis=2, concat_axis=0, tiled=True)  94 us
    all_to_all x1, blocking collectives, body(): lax.all_to_all(local_result, 'state', split_axis=0, concat_axis=2, tiled=...  93.4 us
    all_to_all x2, local copies, waits for them, and re-layouts, body(): lax.all_to_all(head, 'basis', split_axis=2, concat_axis=1, tiled=True)  71.6 us
    all_to_all x1, blocking collectives, body(): lax.all_to_all(lax.all_to_all(local_result, 'state', split_axis=0, concat...  53.1 us
    reshape x1, local copies, waits for them, and re-layouts, body(): head = head.reshape(panel_size, level_count, joint)  49.2 us
    all_to_all x1, waiting for transfers between devices, body(): lax.all_to_all(head, 'basis', split_axis=2, concat_axis=1, tiled=True)  44.5 us
    psum x1, blocking collectives, body(): gram = lax.psum(partial_gram, ('state', 'basis')) / basis_total  42.5 us
  transfers between devices with their start and end apart: 1, of which 1 were waited for; matrix products, arithmetic and copies ran while one was open for 0% of the time, Pallas kernels for 0%

commit v1 on v0

--- a/solution.py
+++ b/solution.py
@@ -1,10 +1,18 @@
+import functools
+
 import jax
 import jax.numpy as jnp
 from jax import lax
+from jax.experimental import pallas as pl
+from jax.experimental.pallas import tpu as pltpu
 from jax.sharding import PartitionSpec as P
 
-
-def body(
+LANES = 128
+GROUP_BLOCKS = 16
+VMEM_LIMIT = 60 * 1024 * 1024
+
+
+def plain_body(
     states, membrane_step, cavity_forward, coupling, membrane_forward, cavity_back, membrane_back
 ):
     highest = lax.Precision.HIGHEST
@@ -51,7 +59,257 @@
     )
 
 
+def split2(x):
+    hi = x.astype(jnp.bfloat16)
+    lo = (x - hi.astype(jnp.float32)).astype(jnp.bfloat16)
+    return hi, lo
+
+
+def bdot(a, b):
+    return jnp.dot(a, b, preferred_element_type=jnp.float32)
+
+
+def left3(wh, wl, x):
+    xh, xl = split2(x)
+    return bdot(jnp.concatenate([wh, wl, wh], axis=1), jnp.concatenate([xh, xh, xl], axis=0))
+
+
+def right3(x, wh, wl):
+    xh, xl = split2(x)
+    return bdot(xh, wh) + bdot(xl, wh) + bdot(xh, wl)
+
+
+def kron_left(w, reps, out_ref_h, out_ref_l):
+    m = w.shape[0]
+    n = m * reps
+    row = lax.broadcasted_iota(jnp.int32, (n, m), 0)
+    col = lax.broadcasted_iota(jnp.int32, (n, m), 1)
+    left = (row // reps == col).astype(jnp.bfloat16)
+    right_row = lax.broadcasted_iota(jnp.int32, (m, n), 0)
+    right_col = lax.broadcasted_iota(jnp.int32, (m, n), 1)
+    right = (right_col // reps == right_row).astype(jnp.bfloat16)
+    a = lax.broadcasted_iota(jnp.int32, (n, n), 0)
+    b = lax.broadcasted_iota(jnp.int32, (n, n), 1)
+    keep = lax.rem(a, reps) == lax.rem(b, reps)
+    for part, ref in zip(split2(w), (out_ref_h, out_ref_l)):
+        full = bdot(bdot(left, part).astype(jnp.bfloat16), right)
+        ref[...] = jnp.where(keep, full, 0.0).astype(jnp.bfloat16)
+
+
+def kron_lanes(w_t, reps, out_ref_h, out_ref_l):
+    m = w_t.shape[0]
+    n = m * reps
+    left = (
+        lax.rem(lax.broadcasted_iota(jnp.int32, (n, m), 0), m)
+        == lax.broadcasted_iota(jnp.int32, (n, m), 1)
+    ).astype(jnp.bfloat16)
+    right = (
+        lax.rem(lax.broadcasted_iota(jnp.int32, (m, n), 1), m)
+        == lax.broadcasted_iota(jnp.int32, (m, n), 0)
+    ).astype(jnp.bfloat16)
+    a = lax.broadcasted_iota(jnp.int32, (n, n), 0)
+    b = lax.broadcasted_iota(jnp.int32, (n, n), 1)
+    keep = a // m == b // m
+    for part, ref in zip(split2(w_t), (out_ref_h, out_ref_l)):
+        full = bdot(bdot(left, part).astype(jnp.bfloat16), right)
+        ref[...] = jnp.where(keep, full, 0.0).astype(jnp.bfloat16)
+
+
+def head_kernel(x_ref, w_ref, o_ref, kh, kl, xs):
+    nb, _, nq, lev, width = o_ref.shape
+    m = w_ref.shape[0]
+    cols = x_ref.shape[2] // m
+
+    @pl.when(pl.program_id(0) == 0)
+    def _():
+        kron_left(w_ref[...], lev, kh, kl)
+        xs[...] = jnp.zeros_like(xs)
+
+    for i in range(m):
+        xs[i * lev : (i + 1) * lev, :cols] = x_ref[0, :, i * cols : (i + 1) * cols]
+    xh, xl = split2(xs[...])
+    y = bdot(kh[...], xh) + bdot(kl[...], xh) + bdot(kh[...], xl)
+    o_ref[...] = y.reshape(nb, 1, nq, lev, width)
+
+
+def step_kernel(x_ref, fc_ref, cp_ref, fk_ref, bc_ref, bk_ref, o_ref, fh, fl, bh, bl, cps, work):
+    nb, ns, _, lev, width = x_ref.shape
+    c_all = fc_ref.shape[0]
+    m = fk_ref.shape[0]
+    group = m * GROUP_BLOCKS
+
+    @pl.when(pl.program_id(0) == 0)
+    def _():
+        kron_lanes(fk_ref[...].T, GROUP_BLOCKS, fh, fl)
+        kron_lanes(bk_ref[...].T, GROUP_BLOCKS, bh, bl)
+        spread = (
+            lax.rem(lax.broadcasted_iota(jnp.int32, (m, group), 1), m)
+            == lax.broadcasted_iota(jnp.int32, (m, group), 0)
+        ).astype(jnp.float32)
+        cps[...] = jnp.dot(cp_ref[...], spread, precision=lax.Precision.HIGHEST)
+
+    ch, cl = split2(fc_ref[...])
+    for s in range(ns):
+        x = x_ref[:, s, 0].reshape(c_all, width)
+        work[s * c_all : (s + 1) * c_all, :] = left3(ch, cl, x)
+    for at in range(0, width, group):
+        n = min(group, width - at)
+        g = right3(work[:, at : at + n], fh[:n, :n], fl[:n, :n])
+        g = (g.reshape(ns, c_all, n) * cps[:, :n][None]).reshape(ns * c_all, n)
+        work[:, at : at + n] = right3(g, bh[:n, :n], bl[:n, :n])
+    dh, dl = split2(bc_ref[...])
+    nz, half = o_ref.shape[0], o_ref.shape[1]
+    for s in range(ns):
+        y = left3(dh, dl, work[s * c_all : (s + 1) * c_all, :])
+        o_ref[:, :, s, 0] = y.reshape(nz, half, lev, width)
+
+
+def gram_kernel(x_ref, o_ref):
+    nz, half, ns, nq, lev, width = x_ref.shape
+    total = nz * ns
+    tiles = width // LANES
+    pairs = [(a, b) for a in range(total) for b in range(a + 1)]
+
+    def outer(hq, accs):
+        h, q = hq // nq, lax.rem(hq, nq)
+        accs = list(accs)
+        for t in range(tiles):
+            vals = [
+                x_ref[a // ns, h, a % ns, q, :, t * LANES : (t + 1) * LANES] for a in range(total)
+            ]
+            for p, (a, b) in enumerate(pairs):
+                accs[p] = accs[p] + vals[a] * vals[b]
+        return tuple(accs)
+
+    zero = jnp.zeros((lev, LANES), jnp.float32)
+    accs = lax.fori_loop(0, half * nq, outer, (zero,) * len(pairs))
+    row = lax.broadcasted_iota(jnp.int32, (total, LANES), 0)
+    col = lax.broadcasted_iota(jnp.int32, (total, LANES), 1)
+    out = jnp.zeros((total, LANES), jnp.float32)
+    for p, (a, b) in enumerate(pairs):
+        v = jnp.sum(jnp.sum(accs[p], axis=0, keepdims=True), axis=1, keepdims=True)
+        here = ((row == a) & (col == b)) | ((row == b) & (col == a))
+        out = jnp.where(here, v, out)
+    o_ref[...] = out
+
+
+def mix_kernel(inv_ref, x_ref, o_ref):
+    nz, half, ns, nq, lev, width = x_ref.shape
+    total = nz * ns
+    for t in range(width // LANES):
+        at = slice(t * LANES, (t + 1) * LANES)
+        vals = [x_ref[a // ns, 0, a % ns, 0, :, at] for a in range(total)]
+        for b in range(total):
+            acc = inv_ref[b, 0] * vals[0]
+            for a in range(1, total):
+                acc = acc + inv_ref[b, a] * vals[a]
+            o_ref[b // ns, 0, b % ns, 0, :, at] = acc
+
+
+def place_kernel(x_ref, o_ref):
+    nb, _, nq, lev, width = x_ref.shape
+    cols = o_ref.shape[2] // (nb * nq)
+    for b in range(nb):
+        for q in range(nq):
+            i = b * nq + q
+            o_ref[0, :, i * cols : (i + 1) * cols] = x_ref[b, 0, q, :, :cols]
+
+
+def fast_body(
+    nz,
+    nb,
+    states,
+    membrane_step,
+    cavity_forward,
+    coupling,
+    membrane_forward,
+    cavity_back,
+    membrane_back,
+):
+    f32 = jnp.float32
+    ns, lev, joint = states.shape
+    m = membrane_step.shape[0]
+    c_all = cavity_forward.shape[0]
+    nq, half = m // nb, nb // nz
+    cols = joint // m
+    width = -(-cols // LANES) * LANES
+    group = m * GROUP_BLOCKS
+    params = pltpu.CompilerParams(vmem_limit_bytes=VMEM_LIMIT)
+    whole = lambda a: pl.BlockSpec(a.shape, lambda *_: (0,) * a.ndim)
+
+    head = pl.pallas_call(
+        head_kernel,
+        grid=(ns,),
+        in_specs=[pl.BlockSpec((1, lev, joint), lambda s: (s, 0, 0)), whole(membrane_step)],
+        out_specs=pl.BlockSpec((nb, 1, nq, lev, width), lambda s: (0, s, 0, 0, 0)),
+        out_shape=jax.ShapeDtypeStruct((nb, ns, nq, lev, width), f32),
+        scratch_shapes=[
+            pltpu.VMEM((m * lev, m * lev), jnp.bfloat16),
+            pltpu.VMEM((m * lev, m * lev), jnp.bfloat16),
+            pltpu.VMEM((m * lev, width), f32),
+        ],
+        compiler_params=params,
+    )(states, membrane_step)
+    block = lax.all_to_all(head, "basis", split_axis=0, concat_axis=0, tiled=True)
+    stepped = pl.pallas_call(
+        step_kernel,
+        grid=(nq,),
+        in_specs=[
+            pl.BlockSpec((nb, ns, 1, lev, width), lambda q: (0, 0, q, 0, 0)),
+            whole(cavity_forward),
+            whole(coupling),
+            whole(membrane_forward),
+            whole(cavity_back),
+            whole(membrane_back),
+        ],
+        out_specs=pl.BlockSpec((nz, half, ns, 1, lev, width), lambda q: (0, 0, 0, q, 0, 0)),
+        out_shape=jax.ShapeDtypeStruct((nz, half, ns, nq, lev, width), f32),
+        scratch_shapes=[pltpu.VMEM((group, group), jnp.bfloat16)] * 4
+        + [pltpu.VMEM((c_all, group), f32), pltpu.VMEM((ns * c_all, width), f32)],
+        compiler_params=params,
+    )(block, cavity_forward, coupling, membrane_forward, cavity_back, membrane_back)
+    spread = lax.all_to_all(stepped, "state", split_axis=0, concat_axis=0, tiled=True)
+    total = nz * ns
+    partial = pl.pallas_call(
+        gram_kernel,
+        out_shape=jax.ShapeDtypeStruct((total, LANES), f32),
+        compiler_params=params,
+    )(spread)
+    gram = lax.psum(partial[:, :total], ("state", "basis")) / float(c_all * joint)
+    lower_factor = jnp.linalg.cholesky(gram)
+    identity = jnp.eye(total, dtype=f32)
+    inverse = lax.linalg.triangular_solve(lower_factor, identity, left_side=True, lower=True)
+    spec = pl.BlockSpec((nz, 1, ns, 1, lev, width), lambda h, q: (0, h, 0, q, 0, 0))
+    mixed = pl.pallas_call(
+        mix_kernel,
+        grid=(half, nq),
+        in_specs=[pl.BlockSpec(memory_space=pltpu.SMEM), spec],
+        out_specs=spec,
+        out_shape=jax.ShapeDtypeStruct(spread.shape, f32),
+        compiler_params=params,
+    )(inverse, spread)
+    back = lax.all_to_all(mixed, "state", split_axis=0, concat_axis=0, tiled=True)
+    back = back.reshape(nb, ns, nq, lev, width)
+    back = lax.all_to_all(back, "basis", split_axis=0, concat_axis=0, tiled=True)
+    return pl.pallas_call(
+        place_kernel,
+        grid=(ns,),
+        in_specs=[pl.BlockSpec((nb, 1, nq, lev, width), lambda s: (0, s, 0, 0, 0))],
+        out_specs=pl.BlockSpec((1, lev, joint), lambda s: (s, 0, 0)),
+        out_shape=jax.ShapeDtypeStruct((ns, lev, joint), f32),
+        compiler_params=params,
+    )(back)
+
+
 def solution(mesh):
+    nz, nb = mesh.shape["state"], mesh.shape["basis"]
     in_specs = (P("state", "basis", None), P(), P(), P(), P(), P(), P())
     out_specs = P("state", "basis", None)
+
+    def body(states, membrane_step, cavity_forward, *rest):
+        m, c_all = membrane_step.shape[0], cavity_forward.shape[0]
+        if m % nb == 0 and nb % nz == 0 and states.shape[1] == 8 and c_all == 8 * nb:
+            return fast_body(nz, nb, states, membrane_step, cavity_forward, *rest)
+        return plain_body(states, membrane_step, cavity_forward, *rest)
+
     return jax.shard_map(body, mesh=mesh, in_specs=in_specs, out_specs=out_specs, check_vma=False)

time: 958 us -> 395 us (0.41); the launches traced: 943 us -> 392 us
  local copies, waits for them, and re-layouts: 515 us -> 1.53 us
  matrix products: 63.7 us -> 0.79 us
  Pallas kernels: 0 us -> 45.4 us
  other arithmetic: 30.9 us -> 2.68 us
    unnamed x19 -> x4, local copies, waits for them, and re-layouts: 302 us -> 1.46 us
    all_to_all x9 -> x0, local copies, waits for them, and re-layouts: 107 us -> none  [the longest x2 71.6 us: body(): lax.all_to_all(head, 'basis', split_axis=2, concat_axis=1, tiled=True)]
    reshape x4 -> x0, local copies, waits for them, and re-layouts: 69.9 us -> none  [the longest x1 49.2 us: body(): head = head.reshape(panel_size, level_count, joint)]
    dot_general x7 -> x0, matrix products: 63.5 us -> none  [the longest x1 13.7 us: body(): jnp.einsum('cq,kqr->kcr', cavity_back, backward, precision=highest)]
    pallas_call x0 -> x5, Pallas kernels: none -> 45.4 us  [the longest x1 20.7 us: fast_body(): pl.pallas_call(step_kernel, grid=(nq,), in_specs=[pl.BlockSpec((nb, ns, 1...]
    all_to_all x2 -> x0, other arithmetic: 28.1 us -> none  [the longest x1 14.4 us: body(): lax.all_to_all(stepped, 'state', split_axis=2, concat_axis=0, tiled=True)]
    dot_general x3 -> x0, local copies, waits for them, and re-layouts: 18.1 us -> none  [the longest x2 9.91 us: body(): local_result = jnp.dot(inverse, flattened, precision=highest)]
    transpose x2 -> x0, local copies, waits for them, and re-layouts: 17.5 us -> none  [the longest x1 10.7 us: body(): jnp.einsum('cq,kqr->kcr', cavity_back, backward, precision=highest)]
where the time goes in v1:
time: 395 us; the launch traced here: 392 us
  blocking collectives  290 us (73%)
  waiting for transfers between devices  45.6 us (12%)
  Pallas kernels  45.4 us (11%)
  starting transfers between devices  5.23 us (1%)
    all_to_all x1, blocking collectives, fast_body(): lax.all_to_all(stepped, 'state', split_axis=0, concat_axis=0, tiled=True)  97.5 us
    all_to_all x1, blocking collectives, fast_body(): lax.all_to_all(mixed, 'state', split_axis=0, concat_axis=0, tiled=True)  96.1 us
    all_to_all x1, blocking collectives, fast_body(): lax.all_to_all(back, 'basis', split_axis=0, concat_axis=0, tiled=True)  54.5 us
    all_to_all x1, waiting for transfers between devices, fast_body(): lax.all_to_all(head, 'basis', split_axis=0, concat_axis=0, tiled=True)  45.6 us
    psum x1, blocking collectives, fast_body(): lax.psum(partial[:, :total], ('state', 'basis')) / float(c_all * joint)  42.4 us
    pallas_call x1, Pallas kernels, fast_body(): pl.pallas_call(step_kernel, grid=(nq,), in_specs=[pl.BlockSpec((nb, ns, 1...  20.7 us
    pallas_call x1, Pallas kernels, fast_body(): pl.pallas_call(mix_kernel, grid=(half, nq), in_specs=[pl.BlockSpec(memory...  8.74 us
  transfers between devices with their start and end apart: 1, of which 1 were waited for; matrix products, arithmetic and copies ran while one was open for 0% of the time, Pallas kernels for 0%

profile of v1, /device:TPU:9, one launch (start us, length us, event | category | flops | bytes accessed | tf_op | source)
XLA Modules:
  0.0 391.8 jit_solution(2096249854357507172)
XLA Ops:
  0.0 7.7 %shard_map.73 = f32[8,2,5,8,1664]{4,3,2,1,0:T(8,128)} custom-call(f32[2,8,64000]{2,1,0:T(8,128)} %x_ref.1, f32[40,40]{1,0:T(8,128)} %w_ref.1), custom_call_target="tpu_custom_call" | custom-call | tf_op jit(solution)/shard_map/pallas_call | solution.py:240
  7.7 0.0 copy-start
  7.7 5.2 %all-to-all-start = ((f32[8,2,5,8,1664]{4,3,2,1,0:T(8,128)}), f32[8,2,5,8,1664]{4,3,2,1,0:T(8,128)}, u32[]{:S(2)}, u32[]{:S(2)}) async-start(f32[8,2,5,8,1664]{4,3,2,1,0:T(8,128)} %shard_map.73), calls=%async_computation | async-start | bytes 8519680 | tf_op jit(solution)/shard_map/all_to_all | solution.py:253
  12.9 0.0 copy-done
  12.9 0.7 copy.8.cp_ref
  13.6 45.6 %all-to-all-done.x_ref = f32[8,2,5,8,1664]{4,3,2,1,0:T(8,128)} async-done(((f32[8,2,5,8,1664]{4,3,2,1,0:T(8,128)}), f32[8,2,5,8,1664]{4,3,2,1,0:T(8,128)}, u32[]{:S(2)}, u32[]{:S(2)}) %all-to-all-start) | async-done | bytes 4259872 | tf_op jit(solution)/shard_map/all_to_all | solution.py:253
  59.2 20.7 %shard_map.74 = f32[4,2,2,5,8,1664]{5,4,3,2,1,0:T(8,128)} custom-call(f32[8,2,5,8,1664]{4,3,2,1,0:T(8,128)} %all-to-all-done.x_ref, f32[64,64]{1,0:T(8,128)} %fc_ref.1, f32[64,40]{1,0:T(8,128)} %copy.8.cp_ref, f32[40,40]{1,0:T(8,128)} %fk_ref.1, f32[64,64]{1,0:T(8,128)} %bc_ref.1, f32[40,40]{1,0:T(8,128)} %bk_ref.1), custom_call_target="tpu_custom_call" | custom-call | tf_op jit(solution)/shard_map/pallas_call | solution.py:254
  80.0 97.5 %all_to_all.20.x_ref = f32[4,2,2,5,8,1664]{5,4,3,2,1,0:T(8,128)} all-to-all(f32[4,2,2,5,8,1664]{5,4,3,2,1,0:T(8,128)} %shard_map.74), channel_id=1, replica_groups=mesh['state'=4,'basis'=8] {'state'}, dimensions={0} | all-to-all | bytes 8519680 | tf_op jit(solution)/shard_map/all_to_all | solution.py:271
  177.4 4.4 %shard_map.75 = f32[8,128]{1,0:T(8,128)} custom-call(f32[4,2,2,5,8,1664]{5,4,3,2,1,0:T(8,128)} %all_to_all.20.x_ref), custom_call_target="tpu_custom_call" | custom-call | tf_op jit(solution)/shard_map/pallas_call | solution.py:273
  181.8 0.8 copy.12
  182.5 42.4 %psum.7 = f32[8,8]{0,1:T(8,128)S(1)} all-reduce(f32[8,8]{0,1:T(8,128)S(1)} %copy.12), channel_id=1, replica_groups=mesh['state'=4,'basis'=8] {'state','basis'}, use_global_device_ids=true, to_apply=%region_0.0 | all-reduce | flops 64 | bytes 512 | tf_op jit(solution)/shard_map/psum | solution.py:278
  225.0 0.1 copy.10
  225.1 0.7 cholesky.17
  225.8 0.6 compare_reduce_fusion
  226.4 0.6 fusion
  227.1 0.6 custom-call.6
  227.7 0.8 fusion.1.inv_ref
  228.5 8.7 %shard_map.76 = f32[4,2,2,5,8,1664]{5,4,3,2,1,0:T(8,128)} custom-call(f32[8,8]{1,0:T(8,128)} %fusion.1.inv_ref, f32[4,2,2,5,8,1664]{5,4,3,2,1,0:T(8,128)} %all_to_all.20.x_ref), custom_call_target="tpu_custom_call" | custom-call | tf_op jit(solution)/shard_map/pallas_call | solution.py:283
  237.3 96.1 %all_to_all.21 = f32[4,2,2,5,8,1664]{5,4,3,2,1,0:T(8,128)S(1)} all-to-all(f32[4,2,2,5,8,1664]{5,4,3,2,1,0:T(8,128)} %shard_map.76), channel_id=1, replica_groups=mesh['state'=4,'basis'=8] {'state'}, dimensions={0} | all-to-all | bytes 8519680 | tf_op jit(solution)/shard_map/all_to_all | solution.py:291
  333.4 54.5 %all_to_all.22.x_ref = f32[8,2,5,8,1664]{4,3,2,1,0:T(8,128)} all-to-all(f32[8,2,5,8,1664]{4,3,2,1,0:T(8,128)S(1)} %bitcast.12), channel_id=1, replica_groups=mesh['state'=4,'basis'=8] {'basis'}, dimensions={0} | all-to-all | bytes 8519680 | tf_op jit(solution)/shard_map/all_to_all | solution.py:293
  387.9 3.9 %shard_map.77 = f32[2,8,64000]{2,1,0:T(8,128)} custom-call(f32[8,2,5,8,1664]{4,3,2,1,0:T(8,128)} %all_to_all.22.x_ref), custom_call_target="tpu_custom_call" | custom-call | tf_op jit(solution)/shard_map/pallas_call | solution.py:294
  (3 shorter events, 0.1 us)
Async XLA Ops:
  7.7 5.2 %copy-start = (f32[64,40]{0,1:T(8,128)S(1)}, f32[64,40]{0,1:T(8,128)}, u32[]{:S(2)}) copy-start(f32[64,40]{0,1:T(8,128)} %param.10) | copy-start | bytes 30724
  7.7 51.5 %all-to-all-start = ((f32[8,2,5,8,1664]{4,3,2,1,0:T(8,128)}), f32[8,2,5,8,1664]{4,3,2,1,0:T(8,128)}, u32[]{:S(2)}, u32[]{:S(2)}) async-start(f32[8,2,5,8,1664]{4,3,2,1,0:T(8,128)} %shard_map.73), calls=%async_computation | async-start | bytes 8519680 | tf_op jit(solution)/shard_map/all_to_all | solution.py:253

commit v2 on v1

--- a/solution.py
+++ b/solution.py
@@ -116,7 +116,7 @@
 
 
 def head_kernel(x_ref, w_ref, o_ref, kh, kl, xs):
-    nb, _, nq, lev, width = o_ref.shape
+    nb, nq, _, lev, width = o_ref.shape
     m = w_ref.shape[0]
     cols = x_ref.shape[2] // m
 
@@ -129,90 +129,314 @@
         xs[i * lev : (i + 1) * lev, :cols] = x_ref[0, :, i * cols : (i + 1) * cols]
     xh, xl = split2(xs[...])
     y = bdot(kh[...], xh) + bdot(kl[...], xh) + bdot(kh[...], xl)
-    o_ref[...] = y.reshape(nb, 1, nq, lev, width)
-
-
-def step_kernel(x_ref, fc_ref, cp_ref, fk_ref, bc_ref, bk_ref, o_ref, fh, fl, bh, bl, cps, work):
-    nb, ns, _, lev, width = x_ref.shape
+    o_ref[...] = y.reshape(nb, nq, 1, lev, width)
+
+
+def remote(src, dst, send_sem, recv_sem, axis, peer):
+    return pltpu.make_async_remote_copy(
+        src_ref=src,
+        dst_ref=dst,
+        send_sem=send_sem,
+        recv_sem=recv_sem,
+        device_id={axis: peer},
+        device_id_type=pl.DeviceIdType.MESH,
+    )
+
+
+def peers_of(axis, size):
+    me = lax.axis_index(axis)
+    return me, [lax.rem(me + d, size) for d in range(1, size)]
+
+
+def state_peers(size):
+    me = lax.axis_index("state")
+    if size != 4:
+        return peers_of("state", size)
+    near = 3 - 2 * lax.rem(me, 2)
+    return me, [lax.rem(me + d, size) for d in (2, near, 4 - near)]
+
+
+def greet(nz, nb):
+    barrier = pltpu.get_barrier_semaphore()
+    for axis, size in (("basis", nb), ("state", nz)):
+        for peer in peers_of(axis, size)[1]:
+            pl.semaphore_signal(
+                barrier, inc=1, device_id={axis: peer}, device_id_type=pl.DeviceIdType.MESH
+            )
+    pl.semaphore_wait(barrier, nb + nz - 2)
+
+
+def gram_tiles(x_ref, q, accs, pairs):
+    nz, half, ns, lev, width = x_ref.shape[1:]
+    accs = list(accs)
+    for h in range(half):
+        for t in range(width // LANES):
+            at = slice(t * LANES, (t + 1) * LANES)
+            vals = [x_ref[q, a // ns, h, a % ns, :, at] for a in range(nz * ns)]
+            for p, (a, b) in enumerate(pairs):
+                accs[p] = accs[p] + vals[a] * vals[b]
+    return tuple(accs)
+
+
+def forward_kernel(
+    nz,
+    nb,
+    x_ref,
+    fc_ref,
+    cp_ref,
+    fk_ref,
+    bc_ref,
+    bk_ref,
+    spread,
+    gram_ref,
+    fh,
+    fl,
+    bh,
+    bl,
+    cps,
+    work,
+    block,
+    stepped,
+    gram_b,
+    gram_z,
+    b_send,
+    b_recv,
+    z_send,
+    z_recv,
+    gb_send,
+    gb_recv,
+    gz_send,
+    gz_recv,
+):
+    _, nq, ns, lev, width = x_ref.shape
+    half = nb // nz
+    total = nz * ns
     c_all = fc_ref.shape[0]
     m = fk_ref.shape[0]
     group = m * GROUP_BLOCKS
-
-    @pl.when(pl.program_id(0) == 0)
-    def _():
-        kron_lanes(fk_ref[...].T, GROUP_BLOCKS, fh, fl)
-        kron_lanes(bk_ref[...].T, GROUP_BLOCKS, bh, bl)
-        spread = (
-            lax.rem(lax.broadcasted_iota(jnp.int32, (m, group), 1), m)
-            == lax.broadcasted_iota(jnp.int32, (m, group), 0)
-        ).astype(jnp.float32)
-        cps[...] = jnp.dot(cp_ref[...], spread, precision=lax.Precision.HIGHEST)
-
+    me_b, others_b = peers_of("basis", nb)
+    me_z, others_z = state_peers(nz)
+
+    def to_basis(q, peer):
+        return remote(
+            x_ref.at[peer, q],
+            block.at[q, me_b],
+            b_send.at[q, peer],
+            b_recv.at[q, me_b],
+            "basis",
+            peer,
+        )
+
+    def from_basis(q, peer):
+        return remote(
+            x_ref.at[me_b, q],
+            block.at[q, peer],
+            b_send.at[q, peer],
+            b_recv.at[q, peer],
+            "basis",
+            peer,
+        )
+
+    def to_state(q, peer):
+        return remote(
+            stepped.at[q, peer],
+            spread.at[q, me_z],
+            z_send.at[q, peer],
+            z_recv.at[q, me_z],
+            "state",
+            peer,
+        )
+
+    def from_state(q, peer):
+        return remote(
+            stepped.at[q, me_z],
+            spread.at[q, peer],
+            z_send.at[q, peer],
+            z_recv.at[q, peer],
+            "state",
+            peer,
+        )
+
+    greet(nz, nb)
+
+    @pl.loop(0, nq)
+    def _(q):
+        for peer in others_b:
+            to_basis(q, peer).start()
+
+    kron_lanes(fk_ref[...].T, GROUP_BLOCKS, fh, fl)
+    kron_lanes(bk_ref[...].T, GROUP_BLOCKS, bh, bl)
+    tile_m = (
+        lax.rem(lax.broadcasted_iota(jnp.int32, (m, group), 1), m)
+        == lax.broadcasted_iota(jnp.int32, (m, group), 0)
+    ).astype(jnp.float32)
+    cps[...] = jnp.dot(cp_ref[...], tile_m, precision=lax.Precision.HIGHEST)
     ch, cl = split2(fc_ref[...])
-    for s in range(ns):
-        x = x_ref[:, s, 0].reshape(c_all, width)
-        work[s * c_all : (s + 1) * c_all, :] = left3(ch, cl, x)
-    for at in range(0, width, group):
-        n = min(group, width - at)
-        g = right3(work[:, at : at + n], fh[:n, :n], fl[:n, :n])
-        g = (g.reshape(ns, c_all, n) * cps[:, :n][None]).reshape(ns * c_all, n)
-        work[:, at : at + n] = right3(g, bh[:n, :n], bl[:n, :n])
     dh, dl = split2(bc_ref[...])
-    nz, half = o_ref.shape[0], o_ref.shape[1]
-    for s in range(ns):
-        y = left3(dh, dl, work[s * c_all : (s + 1) * c_all, :])
-        o_ref[:, :, s, 0] = y.reshape(nz, half, lev, width)
-
-
-def gram_kernel(x_ref, o_ref):
-    nz, half, ns, nq, lev, width = x_ref.shape
-    total = nz * ns
-    tiles = width // LANES
+
+    @pl.loop(0, nq)
+    def _(q):
+        block[q, me_b] = x_ref[me_b, q]
+        for peer in others_b:
+            from_basis(q, peer).wait_recv()
+        for s in range(ns):
+            x = block[q, :, s].reshape(c_all, width)
+            work[s * c_all : (s + 1) * c_all, :] = left3(ch, cl, x)
+        for at in range(0, width, group):
+            n = min(group, width - at)
+            g = right3(work[:, at : at + n], fh[:n, :n], fl[:n, :n])
+            g = (g.reshape(ns, c_all, n) * cps[:, :n][None]).reshape(ns * c_all, n)
+            work[:, at : at + n] = right3(g, bh[:n, :n], bl[:n, :n])
+        for s in range(ns):
+            y = left3(dh, dl, work[s * c_all : (s + 1) * c_all, :])
+            stepped[q, :, :, s] = y.reshape(nz, half, lev, width)
+        for peer in others_z:
+            to_state(q, peer).start()
+        spread[q, me_z] = stepped[q, me_z]
+
     pairs = [(a, b) for a in range(total) for b in range(a + 1)]
 
-    def outer(hq, accs):
-        h, q = hq // nq, lax.rem(hq, nq)
-        accs = list(accs)
-        for t in range(tiles):
-            vals = [
-                x_ref[a // ns, h, a % ns, q, :, t * LANES : (t + 1) * LANES] for a in range(total)
-            ]
-            for p, (a, b) in enumerate(pairs):
-                accs[p] = accs[p] + vals[a] * vals[b]
-        return tuple(accs)
+    def gram_chunk(q, accs):
+        for peer in others_z:
+            from_state(q, peer).wait_recv()
+        return gram_tiles(spread, q, accs, pairs)
 
     zero = jnp.zeros((lev, LANES), jnp.float32)
-    accs = lax.fori_loop(0, half * nq, outer, (zero,) * len(pairs))
+    accs = lax.fori_loop(0, nq, gram_chunk, (zero,) * len(pairs))
     row = lax.broadcasted_iota(jnp.int32, (total, LANES), 0)
     col = lax.broadcasted_iota(jnp.int32, (total, LANES), 1)
-    out = jnp.zeros((total, LANES), jnp.float32)
+    partial = jnp.zeros((total, LANES), jnp.float32)
     for p, (a, b) in enumerate(pairs):
         v = jnp.sum(jnp.sum(accs[p], axis=0, keepdims=True), axis=1, keepdims=True)
         here = ((row == a) & (col == b)) | ((row == b) & (col == a))
-        out = jnp.where(here, v, out)
-    o_ref[...] = out
-
-
-def mix_kernel(inv_ref, x_ref, o_ref):
-    nz, half, ns, nq, lev, width = x_ref.shape
+        partial = jnp.where(here, v, partial)
+
+    def share(slots, send, recv, axis, me, others, value):
+        slots[me] = value
+        for peer in others:
+            remote(slots.at[me], slots.at[me], send.at[peer], recv.at[me], axis, peer).start()
+        for peer in others:
+            remote(slots.at[me], slots.at[peer], send.at[peer], recv.at[peer], axis, peer).wait()
+        out = slots[0]
+        for i in range(1, slots.shape[0]):
+            out = out + slots[i]
+        return out
+
+    partial = share(gram_b, gb_send, gb_recv, "basis", me_b, others_b, partial)
+    gram_ref[...] = share(gram_z, gz_send, gz_recv, "state", me_z, others_z, partial)
+
+    @pl.loop(0, nq)
+    def _(q):
+        for peer in others_b:
+            to_basis(q, peer).wait_send()
+        for peer in others_z:
+            to_state(q, peer).wait_send()
+
+
+def back_kernel(
+    nz, nb, inv_ref, x_ref, o_ref, mixed, held, b_send, b_recv, z_send, z_recv
+):
+    nq, _, half, ns, lev, width = x_ref.shape
     total = nz * ns
-    for t in range(width // LANES):
-        at = slice(t * LANES, (t + 1) * LANES)
-        vals = [x_ref[a // ns, 0, a % ns, 0, :, at] for a in range(total)]
-        for b in range(total):
-            acc = inv_ref[b, 0] * vals[0]
-            for a in range(1, total):
-                acc = acc + inv_ref[b, a] * vals[a]
-            o_ref[b // ns, 0, b % ns, 0, :, at] = acc
+    me_b, others_b = peers_of("basis", nb)
+    me_z, others_z = state_peers(nz)
+
+    def to_state(q, peer):
+        return remote(
+            mixed.at[q, peer],
+            held.at[q, me_z],
+            z_send.at[q, peer],
+            z_recv.at[q, me_z],
+            "state",
+            peer,
+        )
+
+    def from_state(q, peer):
+        return remote(
+            mixed.at[q, me_z],
+            held.at[q, peer],
+            z_send.at[q, peer],
+            z_recv.at[q, peer],
+            "state",
+            peer,
+        )
+
+    def to_basis(q, source, h):
+        peer = source * half + h
+        return remote(
+            held.at[q, source, h],
+            o_ref.at[q, me_b],
+            b_send.at[q, peer],
+            b_recv.at[q, me_b],
+            "basis",
+            peer,
+        )
+
+    def from_basis(q, peer):
+        return remote(
+            held.at[q, 0, 0],
+            o_ref.at[q, peer],
+            b_send.at[q, peer],
+            b_recv.at[q, peer],
+            "basis",
+            peer,
+        )
+
+    greet(nz, nb)
+
+    @pl.loop(0, nq)
+    def _(q):
+        for h in range(half):
+            for t in range(width // LANES):
+                at = slice(t * LANES, (t + 1) * LANES)
+                vals = [x_ref[q, a // ns, h, a % ns, :, at] for a in range(total)]
+                for b in range(total):
+                    acc = inv_ref[b, 0] * vals[0]
+                    for a in range(1, total):
+                        acc = acc + inv_ref[b, a] * vals[a]
+                    mixed[q, b // ns, h, b % ns, :, at] = acc
+        for peer in others_z:
+            to_state(q, peer).start()
+        held[q, me_z] = mixed[q, me_z]
+
+    def hand_on(q, source):
+        for h in range(half):
+            mine = source * half + h == me_b
+
+            @pl.when(jnp.logical_not(mine))
+            def _():
+                to_basis(q, source, h).start()
+
+            @pl.when(mine)
+            def _():
+                o_ref[q, me_b] = held[q, source, h]
+
+    @pl.loop(0, nq)
+    def _(q):
+        hand_on(q, me_z)
+
+    @pl.loop(0, nq)
+    def _(q):
+        for peer in others_z:
+            from_state(q, peer).wait_recv()
+            hand_on(q, peer)
+
+    @pl.loop(0, nq)
+    def _(q):
+        for peer in others_b:
+            from_basis(q, peer).wait_recv()
+            from_basis(q, peer).wait_send()
+        for peer in others_z:
+            to_state(q, peer).wait_send()
 
 
 def place_kernel(x_ref, o_ref):
-    nb, _, nq, lev, width = x_ref.shape
+    nq, nb, _, lev, width = x_ref.shape
     cols = o_ref.shape[2] // (nb * nq)
     for b in range(nb):
         for q in range(nq):
             i = b * nq + q
-            o_ref[0, :, i * cols : (i + 1) * cols] = x_ref[b, 0, q, :, :cols]
+            o_ref[0, :, i * cols : (i + 1) * cols] = x_ref[q, b, 0, :, :cols]
 
 
 def fast_body(
@@ -234,6 +458,9 @@
     cols = joint // m
     width = -(-cols // LANES) * LANES
     group = m * GROUP_BLOCKS
+    total = nz * ns
+    dma = pltpu.SemaphoreType.DMA
+    vmem = pl.BlockSpec(memory_space=pltpu.VMEM)
     params = pltpu.CompilerParams(vmem_limit_bytes=VMEM_LIMIT)
     whole = lambda a: pl.BlockSpec(a.shape, lambda *_: (0,) * a.ndim)
 
@@ -241,8 +468,8 @@
         head_kernel,
         grid=(ns,),
         in_specs=[pl.BlockSpec((1, lev, joint), lambda s: (s, 0, 0)), whole(membrane_step)],
-        out_specs=pl.BlockSpec((nb, 1, nq, lev, width), lambda s: (0, s, 0, 0, 0)),
-        out_shape=jax.ShapeDtypeStruct((nb, ns, nq, lev, width), f32),
+        out_specs=pl.BlockSpec((nb, nq, 1, lev, width), lambda s: (0, 0, s, 0, 0)),
+        out_shape=jax.ShapeDtypeStruct((nb, nq, ns, lev, width), f32),
         scratch_shapes=[
             pltpu.VMEM((m * lev, m * lev), jnp.bfloat16),
             pltpu.VMEM((m * lev, m * lev), jnp.bfloat16),
@@ -250,51 +477,52 @@
         ],
         compiler_params=params,
     )(states, membrane_step)
-    block = lax.all_to_all(head, "basis", split_axis=0, concat_axis=0, tiled=True)
-    stepped = pl.pallas_call(
-        step_kernel,
-        grid=(nq,),
-        in_specs=[
-            pl.BlockSpec((nb, ns, 1, lev, width), lambda q: (0, 0, q, 0, 0)),
-            whole(cavity_forward),
-            whole(coupling),
-            whole(membrane_forward),
-            whole(cavity_back),
-            whole(membrane_back),
+    panel = (nq, nz, half, ns, lev, width)
+    spread, gram = pl.pallas_call(
+        functools.partial(forward_kernel, nz, nb),
+        in_specs=[vmem] * 6,
+        out_specs=[vmem, vmem],
+        out_shape=[
+            jax.ShapeDtypeStruct(panel, f32),
+            jax.ShapeDtypeStruct((total, LANES), f32),
         ],
-        out_specs=pl.BlockSpec((nz, half, ns, 1, lev, width), lambda q: (0, 0, 0, q, 0, 0)),
-        out_shape=jax.ShapeDtypeStruct((nz, half, ns, nq, lev, width), f32),
         scratch_shapes=[pltpu.VMEM((group, group), jnp.bfloat16)] * 4
-        + [pltpu.VMEM((c_all, group), f32), pltpu.VMEM((ns * c_all, width), f32)],
-        compiler_params=params,
-    )(block, cavity_forward, coupling, membrane_forward, cavity_back, membrane_back)
-    spread = lax.all_to_all(stepped, "state", split_axis=0, concat_axis=0, tiled=True)
-    total = nz * ns
-    partial = pl.pallas_call(
-        gram_kernel,
-        out_shape=jax.ShapeDtypeStruct((total, LANES), f32),
-        compiler_params=params,
-    )(spread)
-    gram = lax.psum(partial[:, :total], ("state", "basis")) / float(c_all * joint)
+        + [
+            pltpu.VMEM((c_all, group), f32),
+            pltpu.VMEM((ns * c_all, width), f32),
+            pltpu.VMEM((nq, nb, ns, lev, width), f32),
+            pltpu.VMEM(panel, f32),
+            pltpu.VMEM((nb, total, LANES), f32),
+            pltpu.VMEM((nz, total, LANES), f32),
+        ]
+        + [dma((nq, nb))] * 2
+        + [dma((nq, nz))] * 2
+        + [dma((nb,))] * 2
+        + [dma((nz,))] * 2,
+        compiler_params=pltpu.CompilerParams(
+            vmem_limit_bytes=VMEM_LIMIT, collective_id=0, has_side_effects=True
+        ),
+    )(head, cavity_forward, coupling, membrane_forward, cavity_back, membrane_back)
+    gram = gram[:, :total] / float(c_all * joint)
     lower_factor = jnp.linalg.cholesky(gram)
     identity = jnp.eye(total, dtype=f32)
     inverse = lax.linalg.triangular_solve(lower_factor, identity, left_side=True, lower=True)
-    spec = pl.BlockSpec((nz, 1, ns, 1, lev, width), lambda h, q: (0, h, 0, q, 0, 0))
-    mixed = pl.pallas_call(
-        mix_kernel,
-        grid=(half, nq),
-        in_specs=[pl.BlockSpec(memory_space=pltpu.SMEM), spec],
-        out_specs=spec,
-        out_shape=jax.ShapeDtypeStruct(spread.shape, f32),
-        compiler_params=params,
+    back = pl.pallas_call(
+        functools.partial(back_kernel, nz, nb),
+        in_specs=[pl.BlockSpec(memory_space=pltpu.SMEM), vmem],
+        out_specs=vmem,
+        out_shape=jax.ShapeDtypeStruct((nq, nb, ns, lev, width), f32),
+        scratch_shapes=[pltpu.VMEM(panel, f32)] * 2
+        + [dma((nq, nb))] * 2
+        + [dma((nq, nz))] * 2,
+        compiler_params=pltpu.CompilerParams(
+            vmem_limit_bytes=VMEM_LIMIT, collective_id=1, has_side_effects=True
+        ),
     )(inverse, spread)
-    back = lax.all_to_all(mixed, "state", split_axis=0, concat_axis=0, tiled=True)
-    back = back.reshape(nb, ns, nq, lev, width)
-    back = lax.all_to_all(back, "basis", split_axis=0, concat_axis=0, tiled=True)
     return pl.pallas_call(
         place_kernel,
         grid=(ns,),
-        in_specs=[pl.BlockSpec((nb, 1, nq, lev, width), lambda s: (0, s, 0, 0, 0))],
+        in_specs=[pl.BlockSpec((nq, nb, 1, lev, width), lambda s: (0, 0, s, 0, 0))],
         out_specs=pl.BlockSpec((1, lev, joint), lambda s: (s, 0, 0)),
         out_shape=jax.ShapeDtypeStruct((ns, lev, joint), f32),
         compiler_params=params,

time: 395 us -> 251 us (0.64)
  blocking collectives: 290 us -> 0 us
  Pallas kernels: 45.4 us -> 244 us
  waiting for transfers between devices: 45.6 us -> 0 us
  starting transfers between devices: 5.23 us -> 0 us
    all_to_all x3 -> x0, blocking collectives: 248 us -> none  [the longest x1 97.5 us: fast_body(): lax.all_to_all(stepped, 'state', split_axis=0, concat_axis=0, tiled=True)]
    pallas_call x4 -> x3, Pallas kernels: 37.7 us -> 237 us  [the longest x1 120 us: fast_body(): pl.pallas_call(functools.partial(forward_kernel, nz, nb), in_specs=[vmem]...]
    all_to_all x1 -> x0, waiting for transfers between devices: 45.6 us -> none  [fast_body(): lax.all_to_all(head, 'basis', split_axis=0, concat_axis=0, tiled=True)]
    psum x1 -> x0, blocking collectives: 42.4 us -> none  [fast_body(): lax.psum(partial[:, :total], ('state', 'basis')) / float(c_all * joint)]
    all_to_all x1 -> x0, starting transfers between devices: 5.23 us -> none  [fast_body(): lax.all_to_all(head, 'basis', split_axis=0, concat_axis=0, tiled=True)]
  transfers between devices with their start and end apart: 1 -> 0, of which waited for: 1 -> 0; matrix products, arithmetic and copies ran while one was open for 0% -> 0% of each run, Pallas kernels for 0% -> 0%
where the time goes in v2:
time: 251 us; the launch traced here: 250 us
  Pallas kernels  244 us (97%)
  other arithmetic  2.68 us (1%)
    pallas_call x1, Pallas kernels, fast_body(): pl.pallas_call(functools.partial(forward_kernel, nz, nb), in_specs=[vmem]...  120 us
    pallas_call x1, Pallas kernels, fast_body(): pl.pallas_call(functools.partial(back_kernel, nz, nb), in_specs=[pl.Block...  112 us
    pallas_call x1, Pallas kernels, fast_body(): pl.pallas_call(head_kernel, grid=(ns,), in_specs=[pl.BlockSpec((1, lev, j...  7.69 us

profile of v2, /device:TPU:9, one launch (start us, length us, event | category | flops | bytes accessed | tf_op | source)
XLA Modules:
  0.0 250.3 jit_solution(6145565225165653311)
XLA Ops:
  0.0 1.4 copy.8.cp_ref
  1.4 7.7 %shard_map.73.x_ref = f32[8,5,2,8,1664]{4,3,2,1,0:T(8,128)} custom-call(f32[2,8,64000]{2,1,0:T(8,128)} %x_ref.1, f32[40,40]{1,0:T(8,128)} %w_ref.1), custom_call_target="tpu_custom_call" | custom-call | tf_op jit(solution)/shard_map/pallas_call | solution.py:467
  9.1 120.5 %shard_map.74 = (f32[5,4,2,2,8,1664]{5,4,3,2,1,0:T(8,128)}, f32[8,128]{1,0:T(8,128)}) custom-call(f32[8,5,2,8,1664]{4,3,2,1,0:T(8,128)} %shard_map.73.x_ref, f32[64,64]{1,0:T(8,128)} %fc_ref.1, f32[64,40]{1,0:T(8,128)} %copy.8.cp_ref, f32[40,40]{1,0:T(8,128)} %fk_ref.1, f32[64,64]{1,0:T(8,128)} %bc_ref.1, f32[40,40]{1,0:T(8,128)} %bk_ref.1), custom_call_target="tpu_custom_call" | custom-call | tf_op jit(solution)/shard_map/pallas_call | solution.py:481
  129.6 0.8 copy.9
  130.4 0.1 copy.10
  130.4 0.7 cholesky.17
  131.2 0.6 compare_reduce_fusion
  131.8 0.6 fusion
  132.5 0.6 custom-call.6
  133.1 0.8 fusion.1.inv_ref
  133.9 112.4 %shard_map.75.x_ref = f32[5,8,2,8,1664]{4,3,2,1,0:T(8,128)} custom-call(f32[8,8]{1,0:T(8,128)} %fusion.1.inv_ref, f32[5,4,2,2,8,1664]{5,4,3,2,1,0:T(8,128)} %get-tuple-element.8.x_ref), custom_call_target="tpu_custom_call" | custom-call | tf_op jit(solution)/shard_map/pallas_call | solution.py:510
  246.3 3.9 %shard_map.76 = f32[2,8,64000]{2,1,0:T(8,128)} custom-call(f32[5,8,2,8,1664]{4,3,2,1,0:T(8,128)} %shard_map.75.x_ref), custom_call_target="tpu_custom_call" | custom-call | tf_op jit(solution)/shard_map/pallas_call | solution.py:522
  (3 shorter events, 0.1 us)

commit v3 on v2

v3 whole, which is shorter than its diff:
```python
import functools

import jax
import jax.numpy as jnp
from jax import lax
from jax.experimental import pallas as pl
from jax.experimental.pallas import tpu as pltpu
from jax.sharding import PartitionSpec as P

LANES = 128
GROUP_BLOCKS = 16
VMEM_LIMIT = 60 * 1024 * 1024


def plain_body(
    states, membrane_step, cavity_forward, coupling, membrane_forward, cavity_back, membrane_back
):
    highest = lax.Precision.HIGHEST
    panel_size, level_count, joint = states.shape
    levels_all = cavity_forward.shape[0]
    membrane_levels = membrane_step.shape[0]
    basis_total = float(levels_all * joint)
    head = jnp.einsum(
        "ab,scbr->scar",
        membrane_step,
        states.reshape(panel_size, level_count, membrane_levels, joint // membrane_levels),
        precision=highest,
    )
    head = head.reshape(panel_size, level_count, joint)
    panel_block = lax.all_to_all(head, "basis", split_axis=2, concat_axis=1, tiled=True)
    items, cavity_all, columns = panel_block.shape
    grid = jnp.einsum("qc,kcr->kqr", cavity_forward, panel_block, precision=highest)
    grid = jnp.einsum(
        "kqtm,nm->kqtn",
        grid.reshape(items, cavity_all, columns // membrane_levels, membrane_levels),
        membrane_forward,
        precision=highest,
    )
    weighted = grid * coupling[None, :, None, :]
    backward = jnp.einsum("kqtn,mn->kqtm", weighted, membrane_back, precision=highest)
    backward = backward.reshape(items, cavity_all, columns)
    stepped = jnp.einsum("cq,kqr->kcr", cavity_back, backward, precision=highest)
    spread = lax.all_to_all(stepped, "state", split_axis=2, concat_axis=0, tiled=True)
    state_total, spread_levels, spread_cols = spread.shape
    flattened = spread.reshape(state_total, -1)
    partial_gram = jnp.dot(flattened, flattened.T, precision=highest)
    gram = lax.psum(partial_gram, ("state", "basis")) / basis_total
    lower_factor = jnp.linalg.cholesky(gram)
    identity = jnp.eye(state_total, dtype=gram.dtype)
    inverse = lax.linalg.triangular_solve(lower_factor, identity, left_side=True, lower=True)
    local_result = jnp.dot(inverse, flattened, precision=highest)
    local_result = local_result.reshape(state_total, spread_levels, spread_cols)
    return lax.all_to_all(
        lax.all_to_all(local_result, "state", split_axis=0, concat_axis=2, tiled=True),
        "basis",
        split_axis=1,
        concat_axis=2,
        tiled=True,
    )


def split2(x):
    hi = x.astype(jnp.bfloat16)
    lo = (x - hi.astype(jnp.float32)).astype(jnp.bfloat16)
    return hi, lo


def bdot(a, b):
    return jnp.dot(a, b, preferred_element_type=jnp.float32)


def left3(wh, wl, x):
    xh, xl = split2(x)
    return bdot(jnp.concatenate([wh, wl, wh], axis=1), jnp.concatenate([xh, xh, xl], axis=0))


def right3(x, wh, wl):
    xh, xl = split2(x)
    return bdot(xh, wh) + bdot(xl, wh) + bdot(xh, wl)


def kron_left(w, reps, out_ref_h, out_ref_l):
    m = w.shape[0]
    n = m * reps
    row = lax.broadcasted_iota(jnp.int32, (n, m), 0)
    col = lax.broadcasted_iota(jnp.int32, (n, m), 1)
    left = (row // reps == col).astype(jnp.bfloat16)
    right_row = lax.broadcasted_iota(jnp.int32, (m, n), 0)
    right_col = lax.broadcasted_iota(jnp.int32, (m, n), 1)
    right = (right_col // reps == right_row).astype(jnp.bfloat16)
    a = lax.broadcasted_iota(jnp.int32, (n, n), 0)
    b = lax.broadcasted_iota(jnp.int32, (n, n), 1)
    keep = lax.rem(a, reps) == lax.rem(b, reps)
    for part, ref in zip(split2(w), (out_ref_h, out_ref_l)):
        full = bdot(bdot(left, part).astype(jnp.bfloat16), right)
        ref[...] = jnp.where(keep, full, 0.0).astype(jnp.bfloat16)


def kron_lanes(w_t, reps, out_ref_h, out_ref_l):
    m = w_t.shape[0]
    n = m * reps
    left = (
        lax.rem(lax.broadcasted_iota(jnp.int32, (n, m), 0), m)
        == lax.broadcasted_iota(jnp.int32, (n, m), 1)
    ).astype(jnp.bfloat16)
    right = (
        lax.rem(lax.broadcasted_iota(jnp.int32, (m, n), 1), m)
        == lax.broadcasted_iota(jnp.int32, (m, n), 0)
    ).astype(jnp.bfloat16)
    a = lax.broadcasted_iota(jnp.int32, (n, n), 0)
    b = lax.broadcasted_iota(jnp.int32, (n, n), 1)
    keep = a // m == b // m
    for part, ref in zip(split2(w_t), (out_ref_h, out_ref_l)):
        full = bdot(bdot(left, part).astype(jnp.bfloat16), right)
        ref[...] = jnp.where(keep, full, 0.0).astype(jnp.bfloat16)


def remote(src, dst, send_sem, recv_sem, axis, peer):
    return pltpu.make_async_remote_copy(
        src_ref=src,
        dst_ref=dst,
        send_sem=send_sem,
        recv_sem=recv_sem,
        device_id={axis: peer},
        device_id_type=pl.DeviceIdType.MESH,
    )


def peers_of(axis, size):
    me = lax.axis_index(axis)
    return me, [lax.rem(me + d, size) for d in range(1, size)]


def state_peers(size):
    me = lax.axis_index("state")
    if size != 4:
        return peers_of("state", size)
    near = 3 - 2 * lax.rem(me, 2)
    return me, [lax.rem(me + d, size) for d in (2, near, 4 - near)]


def bulk_tiles(x_ref, q, h, low, nz, ns):
    width = x_ref.shape[-1]
    bulk = (width - LANES) // ns
    for t in range(bulk // LANES):
        yield t, [
            x_ref[q, a // ns, h, :, (a % ns) * bulk + t * LANES : (a % ns) * bulk + (t + 1) * LANES]
            for a in range(nz * ns)
        ]
    vals = []
    for z in range(nz):
        v = x_ref[q, z, h, :, width - LANES :]
        vals += [jnp.where(low, v, 0.0), jnp.where(low, pltpu.roll(v, LANES // 2, 1), 0.0)]
    yield None, vals


def step_kernel(
    nz,
    nb,
    x_ref,
    ms_ref,
    fc_ref,
    cp_ref,
    fk_ref,
    bc_ref,
    bk_ref,
    o_ref,
    xin,
    kh,
    kl,
    xs,
    outgo,
    fh,
    fl,
    bh,
    bl,
    cps,
    work,
    block,
    stepped,
    spread,
    gram_b,
    gram_z,
    splat,
    mixed,
    held,
    in_sem,
    b_send,
    b_recv,
    z_send,
    z_recv,
    gb_send,
    gb_recv,
    gz_send,
    gz_recv,
    y_send,
    y_recv,
    c_send,
    c_recv,
):
    _, nq, ns, lev, width = outgo.shape
    half = nb // nz
    total = nz * ns
    c_all = fc_ref.shape[0]
    m = fk_ref.shape[0]
    cols = x_ref.shape[2] // m
    group = m * GROUP_BLOCKS
    packed = ns * cols
    bulk = (packed - LANES) // ns
    pieces = [pl.ds(0, bulk), pl.ds(bulk, packed - bulk)]
    me_b, others_b = peers_of("basis", nb)
    me_z, others_z = state_peers(nz)
    low = lax.broadcasted_iota(jnp.int32, (lev, LANES), 1) < LANES // 2

    def to_basis(q, s, peer):
        return remote(
            outgo.at[peer, q, s],
            block.at[q, s, me_b],
            b_send.at[q, s, peer],
            b_recv.at[q, s, me_b],
            "basis",
            peer,
        )

    def from_basis(q, s, peer):
        return remote(
            outgo.at[me_b, q, s],
            block.at[q, s, peer],
            b_send.at[q, s, peer],
            b_recv.at[q, s, peer],
            "basis",
            peer,
        )

    def state_out(src, dst, send, recv, q, p, peer):
        return remote(
            src.at[q, peer, :, :, pieces[p]],
            dst.at[q, me_z, :, :, pieces[p]],
            send.at[q, p, peer],
            recv.at[q, p, me_z],
            "state",
            peer,
        )

    def state_in(src, dst, send, recv, q, p, peer):
        return remote(
            src.at[q, me_z, :, :, pieces[p]],
            dst.at[q, peer, :, :, pieces[p]],
            send.at[q, p, peer],
            recv.at[q, p, peer],
            "state",
            peer,
        )

    there = (stepped, spread, z_send, z_recv)
    again = (mixed, held, y_send, y_recv)

    def home_out(q, p, source, h):
        peer = source * half + h
        return remote(
            held.at[q, source, h, :, pieces[p]],
            o_ref.at[q, me_b, :, pieces[p]],
            c_send.at[q, p, peer],
            c_recv.at[q, p, me_b],
            "basis",
            peer,
        )

    def home_in(q, p, peer):
        return remote(
            held.at[q, 0, 0, :, pieces[p]],
            o_ref.at[q, peer, :, pieces[p]],
            c_send.at[q, p, peer],
            c_recv.at[q, p, peer],
            "basis",
            peer,
        )

    barrier = pltpu.get_barrier_semaphore()
    for axis, size in (("basis", nb), ("state", nz)):
        for peer in peers_of(axis, size)[1]:
            pl.semaphore_signal(
                barrier, inc=1, device_id={axis: peer}, device_id_type=pl.DeviceIdType.MESH
            )
    loads = [pltpu.make_async_copy(x_ref.at[s], xin.at[s], in_sem.at[s]) for s in range(ns)]
    for load in loads:
        load.start()
    kron_left(ms_ref[...], lev, kh, kl)
    xs[...] = jnp.zeros_like(xs)
    for s in range(ns):
        loads[s].wait()
        for i in range(m):
            xs[i * lev : (i + 1) * lev, :cols] = xin[s, :, i * cols : (i + 1) * cols]
        xh, xl = split2(xs[...])
        y = bdot(kh[...], xh) + bdot(kl[...], xh) + bdot(kh[...], xl)
        outgo[:, :, s] = y.reshape(nb, nq, lev, width)
        if s == 0:
            pl.semaphore_wait(barrier, nb + nz - 2)
        for peer in others_b:
            to_basis(0, s, peer).start()

    @pl.loop(1, nq)
    def _(q):
        for s in range(ns):
            for peer in others_b:
                to_basis(q, s, peer).start()

    kron_lanes(fk_ref[...].T, GROUP_BLOCKS, fh, fl)
    kron_lanes(bk_ref[...].T, GROUP_BLOCKS, bh, bl)
    tile_m = (
        lax.rem(lax.broadcasted_iota(jnp.int32, (m, group), 1), m)
        == lax.broadcasted_iota(jnp.int32, (m, group), 0)
    ).astype(jnp.float32)
    cps[...] = jnp.dot(cp_ref[...], tile_m, precision=lax.Precision.HIGHEST)
    ch, cl = split2(fc_ref[...])
    dh, dl = split2(bc_ref[...])

    @pl.loop(0, nq)
    def _(q):
        for s in range(ns):
            block[q, s, me_b] = outgo[me_b, q, s]
            for peer in others_b:
                from_basis(q, s, peer).wait_recv()
            work[...] = left3(ch, cl, block[q, s].reshape(c_all, width))
            for at in range(0, width, group):
                n = min(group, width - at)
                g = right3(work[:, at : at + n], fh[:n, :n], fl[:n, :n]) * cps[:, :n]
                work[:, at : at + n] = right3(g, bh[:n, :n], bl[:n, :n])
            y = left3(dh, dl, work[...])
            stepped[q, :, :, :, s * bulk : (s + 1) * bulk] = y[:, :bulk].reshape(
                nz, half, lev, bulk
            )
            tail = y[:, bulk:]
            if s == 0:
                first_tail = tail
            else:
                tail = jnp.where(
                    lax.broadcasted_iota(jnp.int32, tail.shape, 1) < LANES // 2,
                    first_tail,
                    pltpu.roll(tail, LANES // 2, 1),
                )
                stepped[q, :, :, :, packed - LANES :] = tail.reshape(nz, half, lev, LANES)
            for peer in others_z:
                state_out(*there, q, s, peer).start()
        spread[q, me_z] = stepped[q, me_z]

    pairs = [(a, b) for a in range(total) for b in range(a + 1)]

    def gram_chunk(q, accs):
        accs = list(accs)
        for p in range(ns):
            for peer in others_z:
                state_in(*there, q, p, peer).wait_recv()
        for h in range(half):
            for _, vals in bulk_tiles(spread, q, h, low, nz, ns):
                for p, (a, b) in enumerate(pairs):
                    accs[p] = accs[p] + vals[a] * vals[b]
        return tuple(accs)

    zero = jnp.zeros((lev, LANES), jnp.float32)
    accs = lax.fori_loop(0, nq, gram_chunk, (zero,) * len(pairs))
    row = lax.broadcasted_iota(jnp.int32, (total, LANES), 0)
    col = lax.broadcasted_iota(jnp.int32, (total, LANES), 1)
    partial = jnp.zeros((total, LANES), jnp.float32)
    for p, (a, b) in enumerate(pairs):
        v = jnp.sum(jnp.sum(accs[p], axis=0, keepdims=True), axis=1, keepdims=True)
        here = ((row == a) & (col == b)) | ((row == b) & (col == a))
        partial = jnp.where(here, v, partial)

    def share(slots, send, recv, axis, me, others, value):
        slots[me] = value
        for peer in others:
            remote(slots.at[me], slots.at[me], send.at[peer], recv.at[me], axis, peer).start()
        for peer in others:
            remote(slots.at[me], slots.at[peer], send.at[peer], recv.at[peer], axis, peer).wait()
        out = slots[0]
        for i in range(1, slots.shape[0]):
            out = out + slots[i]
        return out

    partial = share(gram_b, gb_send, gb_recv, "basis", me_b, others_b, partial)
    gram = share(gram_z, gz_send, gz_recv, "state", me_z, others_z, partial)
    gram = gram / float(c_all * m * cols)
    pair = jnp.where(col == row + total, 1.0, gram)
    diag = jnp.ones((total, 1), jnp.float32)
    for j in range(total):
        pivot = pair[j : j + 1, j : j + 1]
        diag = jnp.where(row[:, :1] == j, pivot, diag)
        if j < total - 1:
            factor = jnp.where(row[:, :1] > j, pair[:, j : j + 1] / pivot, 0.0)
            pair = pair - factor * pair[j : j + 1, :]
    pair = pair / jnp.sqrt(diag)
    for b in range(total):
        for a in range(total):
            splat[b * total + a] = jnp.broadcast_to(
                pair[b : b + 1, total + a : total + a + 1], (lev, LANES)
            )

    @pl.loop(0, nq)
    def _(q):
        for h in range(half):
            for t, vals in bulk_tiles(spread, q, h, low, nz, ns):
                for z in range(nz):
                    outs = []
                    for b in range(z * ns, (z + 1) * ns):
                        acc = splat[b * total] * vals[0]
                        for a in range(1, total):
                            acc = acc + splat[b * total + a] * vals[a]
                        outs.append(acc)
                    if t is None:
                        mixed[q, z, h, :, packed - LANES :] = jnp.where(
                            low, outs[0], pltpu.roll(outs[1], LANES // 2, 1)
                        )
                    else:
                        for s in range(ns):
                            at = s * bulk + t * LANES
                            mixed[q, z, h, :, at : at + LANES] = outs[s]
        for p in range(ns):
            for peer in others_z:
                state_out(*again, q, p, peer).start()
        held[q, me_z] = mixed[q, me_z]

    def hand_on(q, p, source):
        for h in range(half):
            mine = source * half + h == me_b

            @pl.when(jnp.logical_not(mine))
            def _():
                home_out(q, p, source, h).start()

            @pl.when(mine)
            def _():
                o_ref[q, me_b, :, pieces[p]] = held[q, source, h, :, pieces[p]]

    @pl.loop(0, nq)
    def _(q):
        for p in range(ns):
            hand_on(q, p, me_z)

    @pl.loop(0, nq)
    def _(q):
        for p in range(ns):
            for peer in others_z:
                state_in(*again, q, p, peer).wait_recv()
                hand_on(q, p, peer)

    @pl.loop(0, nq)
    def _(q):
        for p in range(ns):
            for peer in others_b:
                to_basis(q, p, peer).wait_send()
                home_in(q, p, peer).wait_recv()
                home_in(q, p, peer).wait_send()
            for peer in others_z:
                state_out(*there, q, p, peer).wait_send()
                state_out(*again, q, p, peer).wait_send()


def place_kernel(x_ref, o_ref):
    nq, here, lev, packed = x_ref.shape
    ns = o_ref.shape[0]
    cols = packed // ns
    bulk = (packed - LANES) // ns
    rest = cols - bulk
    for b in range(here):
        for q in range(nq):
            for s in range(ns):
                at = (b * nq + q) * cols
                tail = packed - LANES + s * rest
                o_ref[s, :, at : at + bulk] = x_ref[q, b, :, s * bulk : (s + 1) * bulk]
                o_ref[s, :, at + bulk : at + cols] = x_ref[q, b, :, tail : tail + rest]


def fast_body(
    nz,
    nb,
    states,
    membrane_step,
    cavity_forward,
    coupling,
    membrane_forward,
    cavity_back,
    membrane_back,
):
    f32, bf16 = jnp.float32, jnp.bfloat16
    ns, lev, joint = states.shape
    m = membrane_step.shape[0]
    c_all = cavity_forward.shape[0]
    nq, half = m // nb, nb // nz
    cols = joint // m
    width = -(-cols // LANES) * LANES
    group = m * GROUP_BLOCKS
    total = nz * ns
    dma = pltpu.SemaphoreType.DMA
    vmem = pl.BlockSpec(memory_space=pltpu.VMEM)
    panel = (nq, nz, half, lev, ns * cols)
    back = pl.pallas_call(
        functools.partial(step_kernel, nz, nb),
        in_specs=[pl.BlockSpec(memory_space=pl.ANY)] + [vmem] * 6,
        out_specs=vmem,
        out_shape=jax.ShapeDtypeStruct((nq, nb, lev, ns * cols), f32),
        scratch_shapes=[
            pltpu.VMEM((ns, lev, joint), f32),
            pltpu.VMEM((m * lev, m * lev), bf16),
            pltpu.VMEM((m * lev, m * lev), bf16),
            pltpu.VMEM((m * lev, width), f32),
            pltpu.VMEM((nb, nq, ns, lev, width), f32),
        ]
        + [pltpu.VMEM((group, group), bf16)] * 4
        + [
            pltpu.VMEM((c_all, group), f32),
            pltpu.VMEM((c_all, width), f32),
            pltpu.VMEM((nq, ns, nb, lev, width), f32),
            pltpu.VMEM(panel, f32),
            pltpu.VMEM(panel, f32),
            pltpu.VMEM((nb, total, LANES), f32),
            pltpu.VMEM((nz, total, LANES), f32),
            pltpu.VMEM((total * total, lev, LANES), f32),
            pltpu.VMEM(panel, f32),
            pltpu.VMEM(panel, f32),
            dma((ns,)),
        ]
        + [dma((nq, ns, nb))] * 2
        + [dma((nq, ns, nz))] * 2
        + [dma((nb,))] * 2
        + [dma((nz,))] * 2
        + [dma((nq, ns, nz))] * 2
        + [dma((nq, ns, nb))] * 2,
        compiler_params=pltpu.CompilerParams(
            vmem_limit_bytes=VMEM_LIMIT, collective_id=0, has_side_effects=True
        ),
    )(
        states,
        membrane_step,
        cavity_forward,
        coupling,
        membrane_forward,
        cavity_back,
        membrane_back,
    )
    return pl.pallas_call(
        place_kernel,
        grid=(nb // 2,),
        in_specs=[pl.BlockSpec((nq, 2, lev, ns * cols), lambda b: (0, b, 0, 0))],
        out_specs=pl.BlockSpec((ns, lev, 2 * nq * cols), lambda b: (0, 0, b)),
        out_shape=jax.ShapeDtypeStruct((ns, lev, joint), f32),
        compiler_params=pltpu.CompilerParams(vmem_limit_bytes=VMEM_LIMIT),
    )(back)


def solution(mesh):
    nz, nb = mesh.shape["state"], mesh.shape["basis"]
    in_specs = (P("state", "basis", None), P(), P(), P(), P(), P(), P())
    out_specs = P("state", "basis", None)

    def body(states, membrane_step, cavity_forward, *rest):
        m, c_all = membrane_step.shape[0], cavity_forward.shape[0]
        divides = m % nb == 0 and nb % nz == 0 and nb % 2 == 0
        packs = states.shape[0] == 2 and m * m % LANES == LANES // 2
        if divides and packs and states.shape[1] == 8 and c_all == 8 * nb:
            return fast_body(nz, nb, states, membrane_step, cavity_forward, *rest)
        return plain_body(states, membrane_step, cavity_forward, *rest)

    return jax.shard_map(body, mesh=mesh, in_specs=in_specs, out_specs=out_specs, check_vma=False)
```

time: 251 us -> 220 us (0.88)
  Pallas kernels: 244 us -> 218 us
  other arithmetic: 2.68 us -> 0 us
    pallas_call x4 -> x2, Pallas kernels: 244 us -> 218 us  [the longest x1 213 us: fast_body(): pl.pallas_call(functools.partial(step_kernel, nz, nb), in_specs=[pl.Block...]
    another operation x5 -> x0, other arithmetic: 2.67 us -> none  [the longest x3 1.39 us: fast_body(): lower_factor = jnp.linalg.cholesky(gram)]
where the time goes in v3:
time: 220 us
  Pallas kernels  218 us (99%)
    pallas_call x1, Pallas kernels, fast_body(): pl.pallas_call(functools.partial(step_kernel, nz, nb), in_specs=[pl.Block...  213 us
    pallas_call x1, Pallas kernels, fast_body(): pl.pallas_call(place_kernel, grid=(nb // 2,), in_specs=[pl.BlockSpec((nq,...  4.93 us

profile of v3, /device:TPU:9, one launch (start us, length us, event | category | flops | bytes accessed | tf_op | source)
XLA Modules:
  0.0 219.7 jit_solution(2689391905658464806)
XLA Ops:
  0.0 1.4 copy.8.cp_ref
  1.4 213.3 %shard_map.73.x_ref = f32[5,8,8,3200]{3,2,1,0:T(8,128)} custom-call(f32[2,8,64000]{2,1,0:T(8,128)} %x_ref.1, f32[40,40]{1,0:T(8,128)} %ms_ref.1, f32[64,64]{1,0:T(8,128)} %fc_ref.1, f32[64,40]{1,0:T(8,128)} %copy.8.cp_ref, f32[40,40]{1,0:T(8,128)} %fk_ref.1, f32[64,64]{1,0:T(8,128)} %bc_ref.1, f32[40,40]{1,0:T(8,128)} %bk_ref.1), custom_call_target="tpu_custom_call" | custom-call | tf_op jit(solution)/shard_map/pallas_call | solution.py:497
  214.7 4.9 %shard_map.74 = f32[2,8,64000]{2,1,0:T(8,128)} custom-call(f32[5,8,8,3200]{3,2,1,0:T(8,128)} %shard_map.73.x_ref), custom_call_target="tpu_custom_call" | custom-call | tf_op jit(solution)/shard_map/pallas_call | solution.py:541

commit v4 on v3

--- a/solution.py
+++ b/solution.py
@@ -88,8 +88,8 @@
     right_row = lax.broadcasted_iota(jnp.int32, (m, n), 0)
     right_col = lax.broadcasted_iota(jnp.int32, (m, n), 1)
     right = (right_col // reps == right_row).astype(jnp.bfloat16)
-    a = lax.broadcasted_iota(jnp.int32, (n, n), 0)
-    b = lax.broadcasted_iota(jnp.int32, (n, n), 1)
+    a = lax.broadcasted_iota(jnp.int32, (n, 1), 0)
+    b = lax.broadcasted_iota(jnp.int32, (1, n), 1)
     keep = lax.rem(a, reps) == lax.rem(b, reps)
     for part, ref in zip(split2(w), (out_ref_h, out_ref_l)):
         full = bdot(bdot(left, part).astype(jnp.bfloat16), right)
@@ -107,8 +107,8 @@
         lax.rem(lax.broadcasted_iota(jnp.int32, (m, n), 1), m)
         == lax.broadcasted_iota(jnp.int32, (m, n), 0)
     ).astype(jnp.bfloat16)
-    a = lax.broadcasted_iota(jnp.int32, (n, n), 0)
-    b = lax.broadcasted_iota(jnp.int32, (n, n), 1)
+    a = lax.broadcasted_iota(jnp.int32, (n, 1), 0)
+    b = lax.broadcasted_iota(jnp.int32, (1, n), 1)
     keep = a // m == b // m
     for part, ref in zip(split2(w_t), (out_ref_h, out_ref_l)):
         full = bdot(bdot(left, part).astype(jnp.bfloat16), right)
@@ -184,6 +184,7 @@
     splat,
     mixed,
     held,
+    home,
     in_sem,
     b_send,
     b_recv,
@@ -259,7 +260,7 @@
         peer = source * half + h
         return remote(
             held.at[q, source, h, :, pieces[p]],
-            o_ref.at[q, me_b, :, pieces[p]],
+            home.at[q, me_b, :, pieces[p]],
             c_send.at[q, p, peer],
             c_recv.at[q, p, me_b],
             "basis",
@@ -269,7 +270,7 @@
     def home_in(q, p, peer):
         return remote(
             held.at[q, 0, 0, :, pieces[p]],
-            o_ref.at[q, peer, :, pieces[p]],
+            home.at[q, peer, :, pieces[p]],
             c_send.at[q, p, peer],
             c_recv.at[q, p, peer],
             "basis",
@@ -311,7 +312,7 @@
         lax.rem(lax.broadcasted_iota(jnp.int32, (m, group), 1), m)
         == lax.broadcasted_iota(jnp.int32, (m, group), 0)
     ).astype(jnp.float32)
-    cps[...] = jnp.dot(cp_ref[...], tile_m, precision=lax.Precision.HIGHEST)
+    cps[...] = jnp.dot(cp_ref[...].T, tile_m, precision=lax.Precision.HIGHEST)
     ch, cl = split2(fc_ref[...])
     dh, dl = split2(bc_ref[...])
 
@@ -398,24 +399,26 @@
 
     @pl.loop(0, nq)
     def _(q):
-        for h in range(half):
-            for t, vals in bulk_tiles(spread, q, h, low, nz, ns):
-                for z in range(nz):
-                    outs = []
-                    for b in range(z * ns, (z + 1) * ns):
-                        acc = splat[b * total] * vals[0]
-                        for a in range(1, total):
-                            acc = acc + splat[b * total + a] * vals[a]
-                        outs.append(acc)
-                    if t is None:
-                        mixed[q, z, h, :, packed - LANES :] = jnp.where(
-                            low, outs[0], pltpu.roll(outs[1], LANES // 2, 1)
-                        )
-                    else:
-                        for s in range(ns):
-                            at = s * bulk + t * LANES
-                            mixed[q, z, h, :, at : at + LANES] = outs[s]
         for p in range(ns):
+            for h in range(half):
+                for t, vals in bulk_tiles(spread, q, h, low, nz, ns):
+                    if t is None and p < ns - 1:
+                        continue
+                    for z in range(nz):
+                        outs = []
+                        for s in range(ns) if t is None else (p,):
+                            b = z * ns + s
+                            acc = splat[b * total] * vals[0]
+                            for a in range(1, total):
+                                acc = acc + splat[b * total + a] * vals[a]
+                            outs.append(acc)
+                        if t is None:
+                            mixed[q, z, h, :, packed - LANES :] = jnp.where(
+                                low, outs[0], pltpu.roll(outs[1], LANES // 2, 1)
+                            )
+                        else:
+                            at = p * bulk + t * LANES
+                            mixed[q, z, h, :, at : at + LANES] = outs[0]
             for peer in others_z:
                 state_out(*again, q, p, peer).start()
         held[q, me_z] = mixed[q, me_z]
@@ -430,45 +433,42 @@
 
             @pl.when(mine)
             def _():
-                o_ref[q, me_b, :, pieces[p]] = held[q, source, h, :, pieces[p]]
+                home[q, me_b, :, pieces[p]] = held[q, source, h, :, pieces[p]]
 
     @pl.loop(0, nq)
     def _(q):
         for p in range(ns):
             hand_on(q, p, me_z)
 
-    @pl.loop(0, nq)
-    def _(q):
-        for p in range(ns):
-            for peer in others_z:
-                state_in(*again, q, p, peer).wait_recv()
-                hand_on(q, p, peer)
+    def place(q, p):
+        for peer in others_b:
+            home_in(q, p, peer).wait_recv()
+        for b in range(nb):
+            at = (b * nq + q) * cols
+            o_ref[p, :, at : at + bulk] = home[q, b, :, p * bulk : (p + 1) * bulk]
+            if p == ns - 1:
+                for s in range(ns):
+                    tail = packed - LANES + s * (cols - bulk)
+                    o_ref[s, :, at + bulk : at + cols] = home[q, b, :, tail : tail + cols - bulk]
+
+    order = [(q, p) for q in range(nq) for p in range(ns)]
+    for k, (q, p) in enumerate(order):
+        for peer in others_z:
+            state_in(*again, q, p, peer).wait_recv()
+            hand_on(q, p, peer)
+        if k > 0:
+            place(*order[k - 1])
+    place(*order[-1])
 
     @pl.loop(0, nq)
     def _(q):
         for p in range(ns):
             for peer in others_b:
                 to_basis(q, p, peer).wait_send()
-                home_in(q, p, peer).wait_recv()
                 home_in(q, p, peer).wait_send()
             for peer in others_z:
                 state_out(*there, q, p, peer).wait_send()
                 state_out(*again, q, p, peer).wait_send()
-
-
-def place_kernel(x_ref, o_ref):
-    nq, here, lev, packed = x_ref.shape
-    ns = o_ref.shape[0]
-    cols = packed // ns
-    bulk = (packed - LANES) // ns
-    rest = cols - bulk
-    for b in range(here):
-        for q in range(nq):
-            for s in range(ns):
-                at = (b * nq + q) * cols
-                tail = packed - LANES + s * rest
-                o_ref[s, :, at : at + bulk] = x_ref[q, b, :, s * bulk : (s + 1) * bulk]
-                o_ref[s, :, at + bulk : at + cols] = x_ref[q, b, :, tail : tail + rest]
 
 
 def fast_body(
@@ -494,11 +494,11 @@
     dma = pltpu.SemaphoreType.DMA
     vmem = pl.BlockSpec(memory_space=pltpu.VMEM)
     panel = (nq, nz, half, lev, ns * cols)
-    back = pl.pallas_call(
+    return pl.pallas_call(
         functools.partial(step_kernel, nz, nb),
         in_specs=[pl.BlockSpec(memory_space=pl.ANY)] + [vmem] * 6,
         out_specs=vmem,
-        out_shape=jax.ShapeDtypeStruct((nq, nb, lev, ns * cols), f32),
+        out_shape=jax.ShapeDtypeStruct((ns, lev, joint), f32),
         scratch_shapes=[
             pltpu.VMEM((ns, lev, joint), f32),
             pltpu.VMEM((m * lev, m * lev), bf16),
@@ -518,6 +518,7 @@
             pltpu.VMEM((total * total, lev, LANES), f32),
             pltpu.VMEM(panel, f32),
             pltpu.VMEM(panel, f32),
+            pltpu.VMEM((nq, nb, lev, ns * cols), f32),
             dma((ns,)),
         ]
         + [dma((nq, ns, nb))] * 2
@@ -533,19 +534,11 @@
         states,
         membrane_step,
         cavity_forward,
-        coupling,
+        coupling.T,
         membrane_forward,
         cavity_back,
         membrane_back,
     )
-    return pl.pallas_call(
-        place_kernel,
-        grid=(nb // 2,),
-        in_specs=[pl.BlockSpec((nq, 2, lev, ns * cols), lambda b: (0, b, 0, 0))],
-        out_specs=pl.BlockSpec((ns, lev, 2 * nq * cols), lambda b: (0, 0, b)),
-        out_shape=jax.ShapeDtypeStruct((ns, lev, joint), f32),
-        compiler_params=pltpu.CompilerParams(vmem_limit_bytes=VMEM_LIMIT),
-    )(back)
 
 
 def solution(mesh):

time: 220 us -> 218 us (level)
  Pallas kernels: 218 us -> 214 us
  local copies, waits for them, and re-layouts: 1.42 us -> 4.4 us
    pallas_call x1 -> x0, Pallas kernels: 4.93 us -> none  [fast_body(): pl.pallas_call(place_kernel, grid=(nb // 2,), in_specs=[pl.BlockSpec((nq,...]
    unnamed x1, local copies, waits for them, and re-layouts: 1.42 us -> 4.4 us
where the time goes in v4:
time: 218 us
  Pallas kernels  214 us (98%)
  local copies, waits for them, and re-layouts  4.4 us (2%)
    pallas_call x1, Pallas kernels, fast_body(): pl.pallas_call(functools.partial(step_kernel, nz, nb), in_specs=[pl.Block...  214 us
    unnamed x1, local copies, waits for them, and re-layouts  4.4 us

profile of v4, /device:TPU:9, one launch (start us, length us, event | category | flops | bytes accessed | tf_op | source)
XLA Modules:
  0.0 218.0 jit_solution(13933577174222236190)
XLA Ops:
  0.0 213.6 %shard_map.73 = f32[2,8,64000]{2,1,0:T(8,128)} custom-call(f32[2,8,64000]{2,1,0:T(8,128)} %x_ref.1, f32[40,40]{1,0:T(8,128)} %ms_ref.1, f32[64,64]{1,0:T(8,128)} %fc_ref.1, f32[40,64]{1,0:T(8,128)} %bitcast.1, f32[40,40]{1,0:T(8,128)} %fk_ref.1, f32[64,64]{1,0:T(8,128)} %bc_ref.1, f32[40,40]{1,0:T(8,128)} %bk_ref.1), custom_call_target="tpu_custom_call" | custom-call | tf_op jit(solution)/shard_map/pallas_call | solution.py:497
  213.6 4.4 %copy.9 = f32[2,8,64000]{2,1,0:T(8,128)} copy(f32[2,8,64000]{2,1,0:T(8,128)} %shard_map.73) | data formatting | bytes 8192000
